TPU v7x, 256 devices: a whole 4x4x8 slice. The times are simulated.
256 devices in a mesh: kv: 8 (over z_lo, x), bead: 32 (over y, z_hi, core).
Axes of the slice: x: 4, y: 4, z: 8 (z_hi: 4, z_lo: 2; z = z_hi * 2 + z_lo), core: 2. Of those that a mesh axis runs over, the one named last changes fastest.
Arguments:
- miller: int32 [3, 8192], P(None, 'kv'), may hold values from -40 to 40
- lattice_pos: int32 [3, 32768], P(None, ('kv', 'bead')), may hold values from 0 to 4095
- weights: float32 [32, 32768], P(None, ('kv', 'bead')), may hold values from -6 to 6
- observed: float32 [32, 8192], P(None, 'kv'), may hold values from 0.3 to 2
Outputs:
- grad_weights: float32 [32, 32768], P(None, ('kv', 'bead'))
- grad_positions: float32 [3, 32768], P(None, ('kv', 'bead'))
All inputs are finite; a program needn't handle non-finite values.
Results may differ from a plain program's by a relative error of at most 0.0003.
Values sent between devices are 32-bit elements; how exact they have to be, the bound alone decides.
A program may use at most 64 MiB of HBM per device.

v0:
```python
import functools
import math

import jax
import jax.numpy as jnp
from jax import lax
from jax.experimental import pallas as pl
from jax.experimental.pallas import tpu as pltpu
from jax.sharding import PartitionSpec as P

CHANNELS = 32
LATTICE = 4096
BOX_LEN = 64
TWO_PI = 2.0 * math.pi
MESH = pl.DeviceIdType.MESH
BF16 = jnp.bfloat16
F32 = jnp.float32

SIN_POLY = (4.442883014678955, -7.308241367340088, 3.6062889099121094, -0.8457635641098022, 0.10920574516057968)
COS_POLY = (1.4142135381698608, -6.978850841522217, 5.7394609451293945, -1.8835629224777222, 0.31069815158843994)

GROUP = 16
CHUNK = 128
NT = (((1,), (1,)), ((), ()))
NN = (((1,), (0,)), ((), ()))


def poly(u, coefs):
    total = u * coefs[-1] + coefs[-2]
    for c in coefs[-3::-1]:
        total = total * u + c
    return total


def cos_sin(turns):
    f = turns - jnp.round(turns)
    u = f * f
    s = poly(u, SIN_POLY) * f
    c = poly(u, COS_POLY)
    return 1.0 - s * s, s * c


def split(x):
    high = x.astype(BF16)
    return high, (x - high.astype(F32)).astype(BF16)


def dot(a, b, dims):
    return lax.dot_general(a, b, dims, preferred_element_type=F32)


def kernel(
    mil, pos, wts, obs, gw_out, gp_out,
    posbuf, wbuf, mil_t, wsplit, phase, cos_hi, cos_lo, sin_hi, sin_lo,
    amps, shares, coefs, left_cos, left_sin, gw_send, gp_send, gw_recv, gp_recv,
    a_send, a_recv, r_send, r_recv, c_send, c_recv, d_send, d_recv,
):
    kv, bead = lax.axis_index("kv"), lax.axis_index("bead")
    core, yz = lax.rem(bead, 2), bead // 2
    own = kv * 2 + core
    waves = mil.shape[1] // 2
    beads = pos.shape[1]
    half = pl.ds(pl.multiple_of(core * waves, waves), waves)

    def bead_peer(g):
        return (g // 2, yz * 2 + lax.rem(g, 2))

    def wave_peer(j):
        return (kv, j * 2 + core)

    def turned(index, shift):
        return lax.rem(index + shift, GROUP)

    def lanes(g):
        return pl.ds(pl.multiple_of(g * beads, beads), beads)

    def remote(src, dst, send, recv, device):
        return pltpu.make_async_remote_copy(
            src_ref=src, dst_ref=dst, send_sem=send, recv_sem=recv, device_id=device, device_id_type=MESH
        )

    barrier = pltpu.get_barrier_semaphore()
    for s in range(1, GROUP):
        pl.semaphore_signal(barrier, inc=1, device_id=bead_peer(turned(own, s)), device_id_type=MESH)
    for s in range(1, GROUP):
        pl.semaphore_signal(barrier, inc=1, device_id=wave_peer(turned(yz, s)), device_id_type=MESH)

    where = pos[...].astype(F32)
    upper = jnp.floor(where * (1.0 / 64.0))
    lower = where - 64.0 * upper
    posbuf[:, lanes(own)] = jnp.concatenate(
        [upper * (1.0 / 64.0), lower * (1.0 / LATTICE), jnp.zeros((2, beads), F32)], 0
    )
    wbuf[:, lanes(own)] = wts[...]

    pl.semaphore_wait(barrier, 2 * (GROUP - 1))

    pos_copies, wts_copies = [], []
    for s in range(1, GROUP):
        copy = remote(
            posbuf.at[:, lanes(own)], posbuf.at[:, lanes(own)],
            a_send.at[0, s], a_recv.at[0, s], bead_peer(turned(own, s)),
        )
        copy.start()
        pos_copies.append(copy)
    for s in range(1, GROUP):
        copy = remote(
            wbuf.at[:, lanes(own)], wbuf.at[:, lanes(own)],
            a_send.at[1, s], a_recv.at[1, s], bead_peer(turned(own, s)),
        )
        copy.start()
        wts_copies.append(copy)

    index = mil[:, half].astype(F32)
    mil_t[...] = jnp.concatenate([index, index, jnp.zeros((2, waves), F32)], 0).T.astype(BF16)

    for copy in pos_copies:
        copy.wait_recv()
    for copy in wts_copies:
        copy.wait_recv()
    high, low = split(wbuf[...])
    wsplit[...] = jnp.concatenate([high, low], 0)

    rows, columns = 32, 256

    def forward(q, carry):
        first = pl.multiple_of(q * CHUNK, CHUNK)
        phase[...] = dot(mil_t[pl.ds(first, CHUNK), :], posbuf[...].astype(BF16), NN)

        def block(i, inner):
            r = pl.multiple_of(i * rows, rows)
            to = pl.ds(pl.multiple_of(first + r, rows), rows)
            for j in range(phase.shape[1] // columns):
                c = slice(j * columns, (j + 1) * columns)
                co, si = cos_sin(phase[pl.ds(r, rows), c])
                cos_hi[to, c], cos_lo[to, c] = split(co)
                sin_hi[to, c], sin_lo[to, c] = split(si)
            return inner

        lax.fori_loop(0, CHUNK // rows, block, 0)
        here = pl.ds(first, CHUNK)
        for part, (e_hi, e_lo) in enumerate(((cos_hi, cos_lo), (sin_hi, sin_lo))):
            both = dot(wsplit[...], e_hi[here, :], NT)
            amp = both[:CHANNELS] + both[CHANNELS:] + dot(wsplit[:CHANNELS, :], e_lo[here, :], NT)
            for j in range(GROUP):
                amps[j, 2 * part : 2 * part + 1, here] = amp[j : j + 1]
                amps[j, 2 * part + 1 : 2 * part + 2, here] = amp[GROUP + j : GROUP + j + 1]
        for s in range(1, GROUP):
            to = turned(yz, s)
            remote(
                amps.at[to, :, here], shares.at[yz, :, here], r_send.at[q, s], r_recv.at[q, s], wave_peer(to)
            ).start()
        return carry

    lax.fori_loop(0, waves // CHUNK, forward, 0)
    shares[yz] = amps[yz]

    def share_copy(q, s):
        to, here = turned(yz, s), pl.ds(q * CHUNK, CHUNK)
        return remote(
            amps.at[to, :, here], shares.at[yz, :, here], r_send.at[q, s], r_recv.at[q, s], wave_peer(to)
        )

    for q in range(waves // CHUNK):
        for s in range(1, GROUP):
            share_copy(q, s).wait_recv()
    total = shares[0]
    for j in range(1, GROUP):
        total = total + shares[j]
    bead_total = float(CHANNELS * 1024)
    amp_cos, amp_sin = total[0:2], total[2:4]
    measured = jnp.concatenate([obs[pl.ds(yz, 1), half], obs[pl.ds(yz + GROUP, 1), half]], 0)
    residual = (amp_cos * amp_cos + amp_sin * amp_sin) * (1.0 / bead_total) - measured
    scale = residual * (2.0 / bead_total)
    coefs[yz] = jnp.concatenate([scale * amp_cos, scale * amp_sin], 0)

    coef_copies = []
    for s in range(1, GROUP):
        copy = remote(coefs.at[yz], coefs.at[yz], c_send.at[s], c_recv.at[s], wave_peer(turned(yz, s)))
        copy.start()
        coef_copies.append(copy)
    for copy in coef_copies:
        copy.wait_recv()

    every = coefs[...]
    coef_cos = jnp.concatenate([every[:, 0, :], every[:, 1, :]], 0)
    coef_sin = jnp.concatenate([every[:, 2, :], every[:, 3, :]], 0)
    wave_vec = mil[:, half].astype(F32) * (TWO_PI / BOX_LEN)
    for d in range(4):
        if d == 0:
            lc, ls = coef_cos, coef_sin
        else:
            lc, ls = wave_vec[d - 1 : d] * coef_sin, -wave_vec[d - 1 : d] * coef_cos
        for left, value in ((left_cos, lc), (left_sin, ls)):
            hi, lo = split(value)
            left[d * CHANNELS : (d + 1) * CHANNELS, :] = hi
            left[(4 + d) * CHANNELS : (5 + d) * CHANNELS, :] = lo

    wide = 4 * CHANNELS

    def sum_copies(s):
        to = turned(own, s)
        return (
            remote(gw_send.at[to], gw_recv.at[own], d_send.at[0, s], d_recv.at[0, s], bead_peer(to)),
            remote(gp_send.at[to], gp_recv.at[own], d_send.at[1, s], d_recv.at[1, s], bead_peer(to)),
        )

    def backward(i, carry):
        chip = lax.rem(kv + 1 + i, 8)
        at = pl.ds(pl.multiple_of(chip * 2 * beads, 2 * beads), 2 * beads)
        total = None
        for left, e_hi, e_lo in ((left_cos, cos_hi, cos_lo), (left_sin, sin_hi, sin_lo)):
            both = dot(left[...], e_hi[:, at], NN)
            part = both[:wide] + both[wide:] + dot(left[:wide, :], e_lo[:, at], NN)
            total = part if total is None else total + part
        weight = wbuf[:, at]
        comps = [
            jnp.sum(weight * total[CHANNELS * (d + 1) : CHANNELS * (d + 2)], 0, keepdims=True) for d in range(3)
        ]
        comps = jnp.concatenate(comps + [jnp.zeros((1, 2 * beads), F32)], 0)
        for c in range(2):
            g = chip * 2 + c
            gw_send[g] = total[:CHANNELS, c * beads : (c + 1) * beads]
            gp_send[g] = comps[:, c * beads : (c + 1) * beads]

            @pl.when(g != own)
            def _():
                s = lax.rem(g - own + GROUP, GROUP)
                for copy in (
                    remote(gw_send.at[g], gw_recv.at[own], d_send.at[0, s], d_recv.at[0, s], bead_peer(g)),
                    remote(gp_send.at[g], gp_recv.at[own], d_send.at[1, s], d_recv.at[1, s], bead_peer(g)),
                ):
                    copy.start()

        return carry

    lax.fori_loop(0, 8, backward, 0)
    gw_recv[own] = gw_send[own]
    gp_recv[own] = gp_send[own]
    for s in range(1, GROUP):
        for copy in sum_copies(s):
            copy.wait_recv()
    gw, gp = gw_recv[0], gp_recv[0]
    for g in range(1, GROUP):
        gw, gp = gw + gw_recv[g], gp + gp_recv[g]
    gw_out[...] = gw
    gp_out[...] = gp[:3]

    for copy in pos_copies + wts_copies + coef_copies:
        copy.wait_send()
    for s in range(1, GROUP):
        for q in range(waves // CHUNK):
            share_copy(q, s).wait_send()
        for copy in sum_copies(s):
            copy.wait_send()


def per_device(miller, lattice_pos, weights, observed):
    waves, beads = miller.shape[1] // 2, lattice_pos.shape[1]
    many = GROUP * beads
    chunks = waves // CHUNK
    vmem = pl.BlockSpec(memory_space=pltpu.VMEM)
    dma = pltpu.SemaphoreType.DMA
    return pl.pallas_call(
        kernel,
        out_shape=(
            jax.ShapeDtypeStruct((CHANNELS, beads), F32),
            jax.ShapeDtypeStruct((3, beads), F32),
        ),
        in_specs=[vmem] * 4,
        out_specs=[vmem] * 2,
        scratch_shapes=[
            pltpu.VMEM((8, many), F32),
            pltpu.VMEM((CHANNELS, many), F32),
            pltpu.VMEM((waves, 8), BF16),
            pltpu.VMEM((2 * CHANNELS, many), BF16),
            pltpu.VMEM((CHUNK, many), F32),
            pltpu.VMEM((waves, many), BF16),
            pltpu.VMEM((waves, many), BF16),
            pltpu.VMEM((waves, many), BF16),
            pltpu.VMEM((waves, many), BF16),
            pltpu.VMEM((GROUP, 4, waves), F32),
            pltpu.VMEM((GROUP, 4, waves), F32),
            pltpu.VMEM((GROUP, 4, waves), F32),
            pltpu.VMEM((8 * CHANNELS, waves), BF16),
            pltpu.VMEM((8 * CHANNELS, waves), BF16),
            pltpu.VMEM((GROUP, CHANNELS, beads), F32),
            pltpu.VMEM((GROUP, 4, beads), F32),
            pltpu.VMEM((GROUP, CHANNELS, beads), F32),
            pltpu.VMEM((GROUP, 4, beads), F32),
            dma((2, GROUP)),
            dma((2, GROUP)),
            dma((chunks, GROUP)),
            dma((chunks, GROUP)),
            dma((GROUP,)),
            dma((GROUP,)),
            dma((2, GROUP)),
            dma((2, GROUP)),
        ],
        compiler_params=pltpu.CompilerParams(
            collective_id=0, has_side_effects=True, vmem_limit_bytes=48 * 1024 * 1024
        ),
    )(miller, lattice_pos, weights, observed)


def solution(mesh):
    in_specs = (P(None, "kv"), P(None, ("kv", "bead")), P(None, ("kv", "bead")), P(None, "kv"))
    out_specs = (P(None, ("kv", "bead")), P(None, ("kv", "bead")))
    return jax.shard_map(
        per_device, mesh=mesh, in_specs=in_specs, out_specs=out_specs, check_vma=False
    )
```

profile of v0, /device:TPU:1, one launch (start us, length us, event | category | flops | bytes accessed | tf_op | source)
XLA Modules:
  0.0 52.2 jit_solution(9868572275991656336)
XLA Ops:
  0.6 0.0 copy-start
  0.6 0.9 %copy-done = f32[32,1024]{1,0:T(8,128)S(1)} copy-done((f32[32,1024]{1,0:T(8,128)S(1)}, f32[32,1024]{1,0:T(8,128)}, u32[]{:S(2)}) %copy-start) | copy-done | bytes 131096
  1.5 0.0 copy-start.1
  1.5 0.7 %copy-done.1 = s32[3,1024]{1,0:T(4,128)S(1)} copy-done((s32[3,1024]{1,0:T(4,128)S(1)}, s32[3,1024]{1,0:T(4,128)}, u32[]{:S(2)}) %copy-start.1) | copy-done | bytes 12312
  2.3 0.0 copy-start.2
  2.3 0.7 %copy-done.2 = f32[32,128]{1,0:T(8,128)S(1)} copy-done((f32[32,128]{1,0:T(8,128)S(1)}, f32[32,128]{1,0:T(8,128)}, u32[]{:S(2)}) %copy-start.2) | copy-done | bytes 16408
  3.0 0.0 copy-start.3
  3.0 0.7 %copy-done.3 = s32[3,128]{1,0:T(4,128)S(1)} copy-done((s32[3,128]{1,0:T(4,128)S(1)}, s32[3,128]{1,0:T(4,128)}, u32[]{:S(2)}) %copy-start.3) | copy-done | bytes 1560
  3.7 47.3 %shard_map.59 = (f32[32,128]{1,0:T(8,128)S(1)}, f32[3,128]{1,0:T(4,128)S(1)}) custom-call(s32[3,1024]{1,0:T(4,128)S(1)} %copy-done.1, s32[3,128]{1,0:T(4,128)S(1)} %copy-done.3, f32[32,128]{1,0:T(8,128)S(1)} %copy-done.2, f32[32,1024]{1,0:T(8,128)S(1)} %copy-done), custom_call_target="tpu_custom_call" | custom-call | tf_op jit(solution)/shard_map/pallas_call | solution.py:264
  51.0 0.6 %copy.8 = f32[32,128]{1,0:T(8,128)} copy(f32[32,128]{1,0:T(8,128)S(1)} %get-tuple-element.4) | data formatting | bytes 32768
  51.6 0.6 %copy.9 = f32[3,128]{1,0:T(4,128)} copy(f32[3,128]{1,0:T(4,128)S(1)} %get-tuple-element.5) | data formatting | bytes 3072
Async XLA Ops:
  0.6 0.9 %copy-start = (f32[32,1024]{1,0:T(8,128)S(1)}, f32[32,1024]{1,0:T(8,128)}, u32[]{:S(2)}) copy-start(f32[32,1024]{1,0:T(8,128)} %obs.1) | copy-start | bytes 393220
  1.5 0.7 %copy-start.1 = (s32[3,1024]{1,0:T(4,128)S(1)}, s32[3,1024]{1,0:T(4,128)}, u32[]{:S(2)}) copy-start(s32[3,1024]{1,0:T(4,128)} %mil.1) | copy-start | bytes 36868
  2.3 0.7 %copy-start.2 = (f32[32,128]{1,0:T(8,128)S(1)}, f32[32,128]{1,0:T(8,128)}, u32[]{:S(2)}) copy-start(f32[32,128]{1,0:T(8,128)} %wts.1) | copy-start | bytes 49156
  3.0 0.7 %copy-start.3 = (s32[3,128]{1,0:T(4,128)S(1)}, s32[3,128]{1,0:T(4,128)}, u32[]{:S(2)}) copy-start(s32[3,128]{1,0:T(4,128)} %pos.1) | copy-start | bytes 4612
where the time goes:
time: 52.4 us; the launch traced here: 52.2 us
  Pallas kernels  47.3 us (90%)
  local copies, waits for them, and re-layouts  4.2 us (8%)
  between operations  0.65 us (1%)
    pallas_call x1, Pallas kernels, per_device(): pl.pallas_call(kernel, out_shape=(jax.ShapeDtypeStruct((CHANNELS, beads),...  47.3 us
    unnamed x10, local copies, waits for them, and re-layouts  4.2 us

commit v1 on v0

v1 whole, which is shorter than its diff:
```python
import functools
import math

import jax
import jax.numpy as jnp
from jax import lax
from jax.experimental import pallas as pl
from jax.experimental.pallas import tpu as pltpu
from jax.sharding import PartitionSpec as P

CHANNELS = 32
LATTICE = 4096
BOX_LEN = 64
TWO_PI = 2.0 * math.pi
MESH = pl.DeviceIdType.MESH
BF16 = jnp.bfloat16
F32 = jnp.float32

SIN_POLY = (4.442883014678955, -7.308241367340088, 3.6062889099121094, -0.8457635641098022, 0.10920574516057968)
COS_POLY = (1.4142135381698608, -6.978850841522217, 5.7394609451293945, -1.8835629224777222, 0.31069815158843994)

SHARERS = 8
REDUCERS = 32
CHUNK = 256
SLICE = 256
TILES = CHUNK // 128
PIECE = 2 * TILES
FIRST_GROUP = 2
NT = (((1,), (1,)), ((), ()))
NN = (((1,), (0,)), ((), ()))


def poly(u, coefs):
    total = u * coefs[-1] + coefs[-2]
    for c in coefs[-3::-1]:
        total = total * u + c
    return total


def cos_sin(turns):
    f = turns - jnp.round(turns)
    u = f * f
    s = poly(u, SIN_POLY) * f
    c = poly(u, COS_POLY)
    return 1.0 - s * s, s * c


def split(x):
    high = x.astype(BF16)
    return high, (x - high.astype(F32)).astype(BF16)


def dot(a, b, dims):
    return lax.dot_general(a, b, dims, preferred_element_type=F32)


def kernel(
    mil, pos, wts, obs, gw_out, gp_out,
    mil_own, mil_use, pos_own, obs_own, obs_row, obs_send, posbuf, wbuf, mil_t, wsplit,
    even_ch, even_cl, even_sh, even_sl, odd_ch, odd_cl, odd_sh, odd_sl,
    amps, shares, coefs, left_cos, left_sin, grads, gw_send, gp_send, gw_recv, gp_recv,
    in_sem, a_send, a_recv, m_send, m_recv, r_send, r_recv, c_send, c_recv, d_send, d_recv,
    ready, met,
):
    kv, bead = lax.axis_index("kv"), lax.axis_index("bead")
    z_low, x = kv // 4, lax.rem(kv, 4)
    core = lax.rem(bead, 2)
    own = x * 2 + core
    channel = (bead // 8) * 8 + lax.rem(bead // 2, 4) * 2 + z_low
    waves, beads = mil_use.shape[1], pos.shape[1]
    chunks = waves // CHUNK
    chips = SHARERS // 2
    pairs = chips // 2

    def sharer(g):
        return (z_low * 4 + g // 2, (bead // 2) * 2 + lax.rem(g, 2))

    def reducer(r, to_core):
        y, z = r // 8, lax.rem(r, 8)
        return (lax.rem(z, 2) * 4 + x, (y * 4 + z // 2) * 2 + to_core)

    def remote(src, dst, send, recv, device):
        return pltpu.make_async_remote_copy(
            src_ref=src, dst_ref=dst, send_sem=send, recv_sem=recv, device_id=device, device_id_type=MESH
        )

    def greet(device):
        pl.semaphore_signal(barrier, inc=1, device_id=device, device_id_type=MESH)

    def lanes(g):
        return pl.ds(pl.multiple_of(g * beads, beads), beads)

    barrier = pltpu.get_barrier_semaphore()
    for s in range(1, chips):
        greet(sharer(2 * lax.rem(x + s, chips)))

    @pl.when(core == 1)
    def _():
        greet((kv, bead - 1))

    greet(((1 - z_low) * 4 + x, bead - core))
    inputs = [
        pltpu.make_async_copy(src, dst, in_sem.at[i])
        for i, (src, dst) in enumerate(
            ((pos, pos_own), (wts, wbuf.at[:, lanes(own)]), (mil, mil_own), (obs, obs_own))
        )
    ]
    for copy in inputs:
        copy.start()
    for s in range(1, REDUCERS):
        greet(reducer(lax.rem(channel + s, REDUCERS), 1))
    for copy in inputs:
        copy.wait()

    where = pos_own[...].astype(F32)
    upper = jnp.floor(where * (1.0 / 64.0))
    lower = where - 64.0 * upper
    posbuf[:, lanes(own)] = jnp.concatenate(
        [upper * (1.0 / 64.0), lower * (1.0 / LATTICE), jnp.zeros((2, beads), F32)], 0
    )

    def put_row(ref, row):
        for t in range(waves // 128):
            ref[t : t + 1, :] = row[:, t * 128 : (t + 1) * 128]

    @pl.when(core == 0)
    def _():
        put_row(obs_send, obs_own[pl.ds(channel + 1 - 2 * z_low, 1), :])

    @pl.when(core == z_low)
    def _():
        mil_use[...] = mil_own[...]
        put_row(obs_row, obs_own[pl.ds(channel, 1), :])

    @pl.when(core == 0)
    def _():
        pl.semaphore_wait(barrier, SHARERS - 1 + 2)
        pl.semaphore_signal(ready, inc=1, device_id=(kv, bead + 1), device_id_type=MESH)

    @pl.when(core == 1)
    def _():
        pl.semaphore_wait(ready, 1)

    def pos_copy(s):
        g = lax.rem(own + s, SHARERS)
        at = posbuf.at[:, lanes(own)]
        return remote(at, at, a_send.at[0, s], a_recv.at[0, s], sharer(g))

    def wts_copy(s):
        g = lax.rem(own + s, SHARERS)
        at = wbuf.at[:, lanes(own)]
        return remote(at, at, a_send.at[1, s], a_recv.at[1, s], sharer(g))

    beyond = ((1 - z_low) * 4 + x, bead - core + z_low)
    mil_copy = remote(mil_own, mil_use, m_send.at[0], m_recv.at[0], beyond)
    obs_copy = remote(obs_send, obs_row, m_send.at[1], m_recv.at[1], beyond)

    for s in range(1, SHARERS):
        pos_copy(s).start()

    @pl.when(core == 0)
    def _():
        mil_copy.start()
        obs_copy.start()

    for s in range(1, SHARERS):
        wts_copy(s).start()

    @pl.when(core != z_low)
    def _():
        mil_copy.wait_recv()

    index = mil_use[...].astype(F32)
    mil_t[...] = jnp.concatenate([index, index, jnp.zeros((2, waves), F32)], 0).T.astype(BF16)

    for s in range(1, SHARERS):
        pos_copy(s).wait_recv()
    for s in range(1, SHARERS):
        wts_copy(s).wait_recv()
    high, low = split(wbuf[...])
    wsplit[...] = jnp.concatenate([high, low], 0)

    even = ((even_ch, even_cl), (even_sh, even_sl))
    odd = ((odd_ch, odd_cl), (odd_sh, odd_sl))
    rows = 32

    def share_copy(q, r, to):
        src = amps.at[q, pl.ds(pl.multiple_of(to * PIECE, PIECE), PIECE), :]
        dst = shares.at[q, pl.ds(pl.multiple_of(r * PIECE, PIECE), PIECE), :]
        return remote(src, dst, r_send.at[q], r_recv.at[q], reducer(to, core))

    def coef_copy(q, to):
        at = coefs.at[q, pl.ds(pl.multiple_of(channel * PIECE, PIECE), PIECE), :]
        return remote(at, at, c_send.at[q], c_recv.at[q], reducer(to, core))

    def all_pieces(buf, q, send, recv):
        at = buf.at[q, pl.ds(0, (REDUCERS - 1) * PIECE), :]
        return remote(at, at, send.at[q], recv.at[q], reducer(lax.rem(channel + 1, REDUCERS), core))

    def forward(q, carry):
        first = pl.multiple_of(q * CHUNK, CHUNK)
        mine = mil_t[pl.ds(first, CHUNK), :]

        def make(i):
            refs = (even, odd)[i % 2]
            at = slice((i // 2) * SLICE, (i // 2 + 1) * SLICE)
            where = posbuf[:, i * SLICE : (i + 1) * SLICE].astype(BF16)
            turns = dot(mine, where, NN)
            for b in range(CHUNK // rows):
                to = pl.ds(pl.multiple_of(first + b * rows, rows), rows)
                for (hi, lo), value in zip(refs, cos_sin(turns[b * rows : (b + 1) * rows])):
                    hi[to, at], lo[to, at] = split(value)

        def add(i, sums):
            refs = (even, odd)[i % 2]
            at = slice((i // 2) * SLICE, (i // 2 + 1) * SLICE)
            w = wsplit[:, i * SLICE : (i + 1) * SLICE]
            here = pl.ds(first, CHUNK)
            out = []
            for (hi, lo), (both, rest) in zip(refs, sums):
                both = both + dot(w, hi[here, at], NT)
                rest = rest + dot(w[:CHANNELS], lo[here, at], NT)
                out.append((both, rest))
            return out

        slices = SHARERS * beads // SLICE
        sums = [(jnp.zeros((2 * CHANNELS, CHUNK), F32), jnp.zeros((CHANNELS, CHUNK), F32))] * 2
        make(0)
        for i in range(1, slices):
            make(i)
            sums = add(i - 1, sums)
        sums = add(slices - 1, sums)
        for part, (both, rest) in enumerate(sums):
            amp = both[:CHANNELS] + both[CHANNELS:] + rest
            for t in range(TILES):
                amps[q, pl.ds(part * TILES + t, REDUCERS, stride=PIECE), :] = amp[:, t * 128 : (t + 1) * 128]

        @pl.when(jnp.logical_and(q == 0, core == 1))
        def _():
            pl.semaphore_wait(barrier, 2 * (REDUCERS - 1))
            pl.semaphore_signal(met, inc=1, device_id=(kv, bead - 1), device_id_type=MESH)

        @pl.when(jnp.logical_and(q == 0, core == 0))
        def _():
            pl.semaphore_wait(met, 1)

        for s in range(1, REDUCERS):
            share_copy(q, channel, lax.rem(channel + s, REDUCERS)).start()
        own_rows = pl.ds(pl.multiple_of(channel * PIECE, PIECE), PIECE)
        shares[q, own_rows, :] = amps[q, own_rows, :]
        return carry

    lax.fori_loop(0, chunks, forward, 0)

    @pl.when(core != z_low)
    def _():
        obs_copy.wait_recv()

    bead_total = float(CHANNELS * 1024)

    def coefficients(q, carry):
        all_pieces(shares, q, r_send, r_recv).wait_recv()
        total = shares[q, 0:8, :]
        for r in range(8, REDUCERS * PIECE, 8):
            total = total + shares[q, r : r + 8, :]
        total = total[:PIECE] + total[PIECE:]
        amp_cos, amp_sin = total[:TILES], total[TILES:]
        measured = obs_row[pl.ds(q * TILES, TILES), :]
        residual = (amp_cos * amp_cos + amp_sin * amp_sin) * (1.0 / bead_total) - measured
        scale = residual * (2.0 / bead_total)
        own_rows = pl.ds(pl.multiple_of(channel * PIECE, PIECE), PIECE)
        coefs[q, own_rows, :] = jnp.concatenate([scale * amp_cos, scale * amp_sin], 0)
        for s in range(1, REDUCERS):
            coef_copy(q, lax.rem(channel + s, REDUCERS)).start()
        return carry

    lax.fori_loop(0, chunks, coefficients, 0)

    wide = 4 * CHANNELS

    def sum_copies(g, s):
        device = sharer(g)
        return (
            remote(gw_send.at[g], gw_recv.at[own], d_send.at[0, s], d_recv.at[0, s], device),
            remote(gp_send.at[g], gp_recv.at[own], d_send.at[1, s], d_recv.at[1, s], device),
        )

    def backward(begin, end):
        span = slice(begin * CHUNK, end * CHUNK)
        for q in range(begin, end):
            all_pieces(coefs, q, c_send, c_recv).wait_recv()
            for t in range(TILES):
                at = slice(q * CHUNK + t * 128, q * CHUNK + (t + 1) * 128)
                co = coefs[q, pl.ds(t, CHANNELS, stride=PIECE), :]
                si = coefs[q, pl.ds(TILES + t, CHANNELS, stride=PIECE), :]
                vec = mil_use[:, at].astype(F32) * (TWO_PI / BOX_LEN)
                for d in range(4):
                    lc, ls = (co, si) if d == 0 else (vec[d - 1 : d] * si, -vec[d - 1 : d] * co)
                    for left, value in ((left_cos, lc), (left_sin, ls)):
                        hi, lo = split(value)
                        left[d * CHANNELS : (d + 1) * CHANNELS, at] = hi
                        left[(4 + d) * CHANNELS : (5 + d) * CHANNELS, at] = lo

        def pair(i, carry):
            m = lax.rem(x // 2 + 1 + i, pairs)
            at = pl.ds(pl.multiple_of(m * SLICE, SLICE), SLICE)
            for parity, refs in enumerate((even, odd)):
                chip = m * 2 + parity
                to = pl.ds(pl.multiple_of(chip * SLICE, SLICE), SLICE)
                total = None if begin == 0 else grads[:, to]
                for left, (hi, lo) in zip((left_cos, left_sin), refs):
                    both = dot(left[:, span], hi[span, at], NN)
                    part = both[:wide] + both[wide:] + dot(left[:wide, span], lo[span, at], NN)
                    total = part if total is None else total + part
                if end < chunks:
                    grads[:, to] = total
                    continue
                weight = wbuf[:, to]
                comps = [
                    jnp.sum(weight * total[CHANNELS * (d + 1) : CHANNELS * (d + 2)], 0, keepdims=True)
                    for d in range(3)
                ]
                comps = jnp.concatenate(comps + [jnp.zeros((1, SLICE), F32)], 0)
                for c in range(2):
                    g = chip * 2 + c
                    gw_send[g] = total[:CHANNELS, c * beads : (c + 1) * beads]
                    gp_send[g] = comps[:, c * beads : (c + 1) * beads]

                    @pl.when(g != own)
                    def _():
                        for copy in sum_copies(g, lax.rem(g - own + SHARERS, SHARERS)):
                            copy.start()

            return carry

        lax.fori_loop(0, pairs, pair, 0)

    backward(0, FIRST_GROUP)
    backward(FIRST_GROUP, chunks)

    gw_recv[own] = gw_send[own]
    gp_recv[own] = gp_send[own]
    for s in range(1, SHARERS):
        for copy in sum_copies(lax.rem(own + s, SHARERS), s):
            copy.wait_recv()
    gw, gp = gw_recv[0], gp_recv[0]
    for g in range(1, SHARERS):
        gw, gp = gw + gw_recv[g], gp + gp_recv[g]
    gw_out[...] = gw
    gp_out[...] = gp[:3]

    for s in range(1, SHARERS):
        pos_copy(s).wait_send()
        wts_copy(s).wait_send()
        for copy in sum_copies(lax.rem(own + s, SHARERS), s):
            copy.wait_send()
    for q in range(chunks):
        all_pieces(amps, q, r_send, r_recv).wait_send()
        all_pieces(coefs, q, c_send, c_recv).wait_send()

    @pl.when(core == 0)
    def _():
        mil_copy.wait_send()
        obs_copy.wait_send()


def per_device(miller, lattice_pos, weights, observed):
    waves, beads = miller.shape[1], lattice_pos.shape[1]
    many = SHARERS * beads
    chunks = waves // CHUNK
    hbm = pl.BlockSpec(memory_space=pltpu.HBM)
    vmem = pl.BlockSpec(memory_space=pltpu.VMEM)
    dma = pltpu.SemaphoreType.DMA
    pieces = pltpu.VMEM((chunks, REDUCERS * PIECE, 128), F32)
    left = pltpu.VMEM((8 * CHANNELS, waves), BF16)
    sent = [pltpu.VMEM((SHARERS, CHANNELS, beads), F32), pltpu.VMEM((SHARERS, 4, beads), F32)]
    return pl.pallas_call(
        kernel,
        out_shape=(
            jax.ShapeDtypeStruct((CHANNELS, beads), F32),
            jax.ShapeDtypeStruct((3, beads), F32),
        ),
        in_specs=[hbm] * 4,
        out_specs=[vmem] * 2,
        scratch_shapes=[
            pltpu.VMEM(miller.shape, jnp.int32),
            pltpu.VMEM(miller.shape, jnp.int32),
            pltpu.VMEM(lattice_pos.shape, jnp.int32),
            pltpu.VMEM(observed.shape, F32),
            pltpu.VMEM((waves // 128, 128), F32),
            pltpu.VMEM((waves // 128, 128), F32),
            pltpu.VMEM((8, many), F32),
            pltpu.VMEM((CHANNELS, many), F32),
            pltpu.VMEM((waves, 8), BF16),
            pltpu.VMEM((2 * CHANNELS, many), BF16),
        ]
        + [pltpu.VMEM((waves, many // 2), BF16)] * 8
        + [pieces] * 3
        + [left] * 2
        + [pltpu.VMEM((4 * CHANNELS, many), F32)]
        + sent * 2
        + [
            dma((4,)),
            dma((2, SHARERS)),
            dma((2, SHARERS)),
            dma((2,)),
            dma((2,)),
            dma((chunks,)),
            dma((chunks,)),
            dma((chunks,)),
            dma((chunks,)),
            dma((2, SHARERS)),
            dma((2, SHARERS)),
            pltpu.SemaphoreType.REGULAR,
            pltpu.SemaphoreType.REGULAR,
        ],
        compiler_params=pltpu.CompilerParams(
            collective_id=0, has_side_effects=True, vmem_limit_bytes=56 * 1024 * 1024
        ),
    )(miller, lattice_pos, weights, observed)


def solution(mesh):
    in_specs = (P(None, "kv"), P(None, ("kv", "bead")), P(None, ("kv", "bead")), P(None, "kv"))
    out_specs = (P(None, ("kv", "bead")), P(None, ("kv", "bead")))
    return jax.shard_map(
        per_device, mesh=mesh, in_specs=in_specs, out_specs=out_specs, check_vma=False
    )
```

time: 52.4 us -> 42.4 us (0.81)
  Pallas kernels: 47.3 us -> 39.7 us
  local copies, waits for them, and re-layouts: 4.2 us -> 1.91 us
    pallas_call x1, Pallas kernels: 47.3 us -> 39.7 us  [per_device(): pl.pallas_call(kernel, out_shape=(jax.ShapeDtypeStruct((CHANNELS, beads),...]
    unnamed x10 -> x4, local copies, waits for them, and re-layouts: 4.2 us -> 1.91 us
where the time goes in v1:
time: 42.4 us; the launch traced here: 42.3 us
  Pallas kernels  39.7 us (94%)
  local copies, waits for them, and re-layouts  1.91 us (5%)
  between operations  0.65 us (2%)
    pallas_call x1, Pallas kernels, per_device(): pl.pallas_call(kernel, out_shape=(jax.ShapeDtypeStruct((CHANNELS, beads),...  39.7 us
    unnamed x4, local copies, waits for them, and re-layouts  1.91 us

profile of v1, /device:TPU:1, one launch (start us, length us, event | category | flops | bytes accessed | tf_op | source)
XLA Modules:
  0.0 42.3 jit_solution(6821894526610368719)
XLA Ops:
  0.6 39.7 %shard_map.59 = (f32[32,128]{1,0:T(8,128)}, f32[3,128]{1,0:T(4,128)}) custom-call(s32[3,1024]{1,0:T(4,128)} %mil.1, s32[3,128]{1,0:T(4,128)} %pos.1, f32[32,128]{1,0:T(8,128)} %wts.1, f32[32,1024]{1,0:T(8,128)} %obs.1), custom_call_target="tpu_custom_call" | custom-call | tf_op jit(solution)/shard_map/pallas_call | solution.py:377
  40.3 0.0 copy-start
  40.4 1.3 %copy.8 = f32[32,128]{1,0:T(8,128)} copy(f32[32,128]{1,0:T(8,128)} %get-tuple-element.4) | data formatting | bytes 32768
  41.7 0.0 copy-done
  41.7 0.6 %copy.9 = f32[3,128]{1,0:T(4,128)} copy(f32[3,128]{1,0:T(4,128)S(1)} %copy-done) | data formatting | bytes 3072
Async XLA Ops:
  40.3 1.3 %copy-start = (f32[3,128]{1,0:T(4,128)S(1)}, f32[3,128]{1,0:T(4,128)}, u32[]{:S(2)}) copy-start(f32[3,128]{1,0:T(4,128)} %get-tuple-element.5) | copy-start | bytes 4612

commit v2 on v1

--- a/solution.py
+++ b/solution.py
@@ -11,6 +11,7 @@
 CHANNELS = 32
 LATTICE = 4096
 BOX_LEN = 64
+BEADS = 32768
 TWO_PI = 2.0 * math.pi
 MESH = pl.DeviceIdType.MESH
 BF16 = jnp.bfloat16
@@ -25,7 +26,6 @@
 SLICE = 256
 TILES = CHUNK // 128
 PIECE = 2 * TILES
-FIRST_GROUP = 2
 NT = (((1,), (1,)), ((), ()))
 NN = (((1,), (0,)), ((), ()))
 
@@ -56,9 +56,9 @@
 
 def kernel(
     mil, pos, wts, obs, gw_out, gp_out,
-    mil_own, mil_use, pos_own, obs_own, obs_row, obs_send, posbuf, wbuf, mil_t, wsplit,
-    even_ch, even_cl, even_sh, even_sl, odd_ch, odd_cl, odd_sh, odd_sl,
-    amps, shares, coefs, left_cos, left_sin, grads, gw_send, gp_send, gw_recv, gp_recv,
+    mil_own, mil_use, pos_own, obs_own, obs_row, obs_send, posbuf, wbuf, mil_rows, pos_t, wsplit,
+    hi_a, lo_a, hi_b, lo_b, phase,
+    amps, shares, coefs, left, grads, gw_send, gp_send, gw_recv, gp_recv,
     in_sem, a_send, a_recv, m_send, m_recv, r_send, r_recv, c_send, c_recv, d_send, d_recv,
     ready, met,
 ):
@@ -70,7 +70,6 @@
     waves, beads = mil_use.shape[1], pos.shape[1]
     chunks = waves // CHUNK
     chips = SHARERS // 2
-    pairs = chips // 2
 
     def sharer(g):
         return (z_low * 4 + g // 2, (bead // 2) * 2 + lax.rem(g, 2))
@@ -107,8 +106,6 @@
     ]
     for copy in inputs:
         copy.start()
-    for s in range(1, REDUCERS):
-        greet(reducer(lax.rem(channel + s, REDUCERS), 1))
     for copy in inputs:
         copy.wait()
 
@@ -165,23 +162,21 @@
 
     for s in range(1, SHARERS):
         wts_copy(s).start()
+    for s in range(1, REDUCERS):
+        greet(reducer(lax.rem(channel + s, REDUCERS), 1))
 
     @pl.when(core != z_low)
     def _():
         mil_copy.wait_recv()
 
     index = mil_use[...].astype(F32)
-    mil_t[...] = jnp.concatenate([index, index, jnp.zeros((2, waves), F32)], 0).T.astype(BF16)
+    mil_rows[...] = jnp.concatenate([index, index, jnp.zeros((2, waves), F32)], 0).astype(BF16)
 
     for s in range(1, SHARERS):
         pos_copy(s).wait_recv()
-    for s in range(1, SHARERS):
-        wts_copy(s).wait_recv()
-    high, low = split(wbuf[...])
-    wsplit[...] = jnp.concatenate([high, low], 0)
-
-    even = ((even_ch, even_cl), (even_sh, even_sl))
-    odd = ((odd_ch, odd_cl), (odd_sh, odd_sl))
+    pos_t[...] = posbuf[...].T.astype(BF16)
+
+    sets = ((hi_a, lo_a), (hi_b, lo_b))
     rows = 32
 
     def share_copy(q, r, to):
@@ -197,66 +192,69 @@
         at = buf.at[q, pl.ds(0, (REDUCERS - 1) * PIECE), :]
         return remote(at, at, send.at[q], recv.at[q], reducer(lax.rem(channel + 1, REDUCERS), core))
 
-    def forward(q, carry):
-        first = pl.multiple_of(q * CHUNK, CHUNK)
-        mine = mil_t[pl.ds(first, CHUNK), :]
-
-        def make(i):
-            refs = (even, odd)[i % 2]
-            at = slice((i // 2) * SLICE, (i // 2 + 1) * SLICE)
-            where = posbuf[:, i * SLICE : (i + 1) * SLICE].astype(BF16)
-            turns = dot(mine, where, NN)
-            for b in range(CHUNK // rows):
-                to = pl.ds(pl.multiple_of(first + b * rows, rows), rows)
-                for (hi, lo), value in zip(refs, cos_sin(turns[b * rows : (b + 1) * rows])):
-                    hi[to, at], lo[to, at] = split(value)
-
-        def add(i, sums):
-            refs = (even, odd)[i % 2]
-            at = slice((i // 2) * SLICE, (i // 2 + 1) * SLICE)
-            w = wsplit[:, i * SLICE : (i + 1) * SLICE]
-            here = pl.ds(first, CHUNK)
-            out = []
-            for (hi, lo), (both, rest) in zip(refs, sums):
-                both = both + dot(w, hi[here, at], NT)
-                rest = rest + dot(w[:CHANNELS], lo[here, at], NT)
-                out.append((both, rest))
-            return out
-
-        slices = SHARERS * beads // SLICE
-        sums = [(jnp.zeros((2 * CHANNELS, CHUNK), F32), jnp.zeros((CHANNELS, CHUNK), F32))] * 2
-        make(0)
-        for i in range(1, slices):
-            make(i)
-            sums = add(i - 1, sums)
-        sums = add(slices - 1, sums)
-        for part, (both, rest) in enumerate(sums):
-            amp = both[:CHANNELS] + both[CHANNELS:] + rest
-            for t in range(TILES):
-                amps[q, pl.ds(part * TILES + t, REDUCERS, stride=PIECE), :] = amp[:, t * 128 : (t + 1) * 128]
-
-        @pl.when(jnp.logical_and(q == 0, core == 1))
-        def _():
-            pl.semaphore_wait(barrier, 2 * (REDUCERS - 1))
-            pl.semaphore_signal(met, inc=1, device_id=(kv, bead - 1), device_id_type=MESH)
-
-        @pl.when(jnp.logical_and(q == 0, core == 0))
-        def _():
-            pl.semaphore_wait(met, 1)
-
+    def add(q, turn, base):
+        hi, lo = sets[turn]
+        at = pl.ds(base, 2 * CHUNK)
+        both = dot(wsplit[...], hi[:, at], NN)
+        amp = both[:CHANNELS] + both[CHANNELS:] + dot(wsplit[:CHANNELS, :], lo[:, at], NN)
+        for t in range(PIECE):
+            amps[q, pl.ds(t, REDUCERS, stride=PIECE), :] = amp[:, t * 128 : (t + 1) * 128]
+
+    def make(q, turn, base):
+        hi, lo = sets[turn]
+        phase[...] = dot(pos_t[...], mil_rows[:, pl.ds(pl.multiple_of(q * CHUNK, CHUNK), CHUNK)], NN)
+        for r in range(0, phase.shape[0], rows):
+            for part, value in enumerate(cos_sin(phase[r : r + rows, :])):
+                at = pl.ds(pl.multiple_of(base + part * CHUNK, CHUNK), CHUNK)
+                hi[r : r + rows, at], lo[r : r + rows, at] = split(value)
+
+    def send_shares(q):
         for s in range(1, REDUCERS):
             share_copy(q, channel, lax.rem(channel + s, REDUCERS)).start()
         own_rows = pl.ds(pl.multiple_of(channel * PIECE, PIECE), PIECE)
         shares[q, own_rows, :] = amps[q, own_rows, :]
+
+    def forward(h, carry):
+        base = pl.multiple_of(h * 2 * CHUNK, 2 * CHUNK)
+        before = pl.multiple_of(jnp.maximum(h - 1, 0) * 2 * CHUNK, 2 * CHUNK)
+        add(lax.rem(2 * h + chunks - 1, chunks), 1, before)
+        make(2 * h, 0, base)
+
+        @pl.when(h > 0)
+        def _():
+            send_shares(2 * h - 1)
+
+        @pl.when(h == 0)
+        def _():
+            for s in range(1, SHARERS):
+                wts_copy(s).wait_recv()
+            high, low = split(wbuf[...])
+            wsplit[...] = jnp.concatenate([high, low], 0)
+
+        add(2 * h, 0, base)
+        make(2 * h + 1, 1, base)
+
+        @pl.when(jnp.logical_and(h == 0, core == 1))
+        def _():
+            pl.semaphore_wait(barrier, 2 * (REDUCERS - 1))
+            pl.semaphore_signal(met, inc=1, device_id=(kv, bead - 1), device_id_type=MESH)
+
+        @pl.when(jnp.logical_and(h == 0, core == 0))
+        def _():
+            pl.semaphore_wait(met, 1)
+
+        send_shares(2 * h)
         return carry
 
-    lax.fori_loop(0, chunks, forward, 0)
+    lax.fori_loop(0, chunks // 2, forward, 0)
+    add(chunks - 1, 1, (chunks // 2 - 1) * 2 * CHUNK)
+    send_shares(chunks - 1)
 
     @pl.when(core != z_low)
     def _():
         obs_copy.wait_recv()
 
-    bead_total = float(CHANNELS * 1024)
+    bead_total = float(BEADS)
 
     def coefficients(q, carry):
         all_pieces(shares, q, r_send, r_recv).wait_recv()
@@ -285,9 +283,8 @@
             remote(gp_send.at[g], gp_recv.at[own], d_send.at[1, s], d_recv.at[1, s], device),
         )
 
-    def backward(begin, end):
-        span = slice(begin * CHUNK, end * CHUNK)
-        for q in range(begin, end):
+    def backward(h):
+        for q in (2 * h, 2 * h + 1):
             all_pieces(coefs, q, c_send, c_recv).wait_recv()
             for t in range(TILES):
                 at = slice(q * CHUNK + t * 128, q * CHUNK + (t + 1) * 128)
@@ -296,47 +293,47 @@
                 vec = mil_use[:, at].astype(F32) * (TWO_PI / BOX_LEN)
                 for d in range(4):
                     lc, ls = (co, si) if d == 0 else (vec[d - 1 : d] * si, -vec[d - 1 : d] * co)
-                    for left, value in ((left_cos, lc), (left_sin, ls)):
+                    for part, value in ((0, lc), (1, ls)):
                         hi, lo = split(value)
-                        left[d * CHANNELS : (d + 1) * CHANNELS, at] = hi
-                        left[(4 + d) * CHANNELS : (5 + d) * CHANNELS, at] = lo
-
-        def pair(i, carry):
-            m = lax.rem(x // 2 + 1 + i, pairs)
-            at = pl.ds(pl.multiple_of(m * SLICE, SLICE), SLICE)
-            for parity, refs in enumerate((even, odd)):
-                chip = m * 2 + parity
-                to = pl.ds(pl.multiple_of(chip * SLICE, SLICE), SLICE)
-                total = None if begin == 0 else grads[:, to]
-                for left, (hi, lo) in zip((left_cos, left_sin), refs):
-                    both = dot(left[:, span], hi[span, at], NN)
-                    part = both[:wide] + both[wide:] + dot(left[:wide, span], lo[span, at], NN)
-                    total = part if total is None else total + part
-                if end < chunks:
-                    grads[:, to] = total
-                    continue
-                weight = wbuf[:, to]
-                comps = [
-                    jnp.sum(weight * total[CHANNELS * (d + 1) : CHANNELS * (d + 2)], 0, keepdims=True)
-                    for d in range(3)
-                ]
-                comps = jnp.concatenate(comps + [jnp.zeros((1, SLICE), F32)], 0)
-                for c in range(2):
-                    g = chip * 2 + c
-                    gw_send[g] = total[:CHANNELS, c * beads : (c + 1) * beads]
-                    gp_send[g] = comps[:, c * beads : (c + 1) * beads]
-
-                    @pl.when(g != own)
-                    def _():
-                        for copy in sum_copies(g, lax.rem(g - own + SHARERS, SHARERS)):
-                            copy.start()
+                        first = (2 * (q - 2 * h) + part) * CHUNK + t * 128
+                        to = slice(first, first + 128)
+                        left[d * CHANNELS : (d + 1) * CHANNELS, to] = hi
+                        left[(4 + d) * CHANNELS : (5 + d) * CHANNELS, to] = lo
+
+        span = slice(h * 2 * CHUNK, (h + 1) * 2 * CHUNK)
+
+        def one_chip(i, carry):
+            chip = lax.rem(x + 1 + i, chips)
+            at = pl.ds(pl.multiple_of(chip * SLICE, SLICE), SLICE)
+            both = dot(left[...], jnp.concatenate([hi_a[at, span], hi_b[at, span]], 1), NT)
+            rest = dot(left[:wide, :], jnp.concatenate([lo_a[at, span], lo_b[at, span]], 1), NT)
+            total = both[:wide] + both[wide:] + rest
+            if h > 0:
+                total = total + grads[:, at]
+            if h < chunks // 2 - 1:
+                grads[:, at] = total
+                return carry
+            weight = wbuf[:, at]
+            comps = [
+                jnp.sum(weight * total[CHANNELS * (d + 1) : CHANNELS * (d + 2)], 0, keepdims=True) for d in range(3)
+            ]
+            comps = jnp.concatenate(comps + [jnp.zeros((1, SLICE), F32)], 0)
+            for c in range(2):
+                g = chip * 2 + c
+                gw_send[g] = total[:CHANNELS, c * beads : (c + 1) * beads]
+                gp_send[g] = comps[:, c * beads : (c + 1) * beads]
+
+                @pl.when(g != own)
+                def _():
+                    for copy in sum_copies(g, lax.rem(g - own + SHARERS, SHARERS)):
+                        copy.start()
 
             return carry
 
-        lax.fori_loop(0, pairs, pair, 0)
-
-    backward(0, FIRST_GROUP)
-    backward(FIRST_GROUP, chunks)
+        lax.fori_loop(0, chips, one_chip, 0)
+
+    for h in range(chunks // 2):
+        backward(h)
 
     gw_recv[own] = gw_send[own]
     gp_recv[own] = gp_send[own]
@@ -372,7 +369,6 @@
     vmem = pl.BlockSpec(memory_space=pltpu.VMEM)
     dma = pltpu.SemaphoreType.DMA
     pieces = pltpu.VMEM((chunks, REDUCERS * PIECE, 128), F32)
-    left = pltpu.VMEM((8 * CHANNELS, waves), BF16)
     sent = [pltpu.VMEM((SHARERS, CHANNELS, beads), F32), pltpu.VMEM((SHARERS, 4, beads), F32)]
     return pl.pallas_call(
         kernel,
@@ -391,13 +387,14 @@
             pltpu.VMEM((waves // 128, 128), F32),
             pltpu.VMEM((8, many), F32),
             pltpu.VMEM((CHANNELS, many), F32),
-            pltpu.VMEM((waves, 8), BF16),
+            pltpu.VMEM((8, waves), BF16),
+            pltpu.VMEM((many, 8), BF16),
             pltpu.VMEM((2 * CHANNELS, many), BF16),
         ]
-        + [pltpu.VMEM((waves, many // 2), BF16)] * 8
+        + [pltpu.VMEM((many, waves), BF16)] * 4
+        + [pltpu.VMEM((many, CHUNK), F32)]
         + [pieces] * 3
-        + [left] * 2
-        + [pltpu.VMEM((4 * CHANNELS, many), F32)]
+        + [pltpu.VMEM((8 * CHANNELS, 4 * CHUNK), BF16), pltpu.VMEM((4 * CHANNELS, many), F32)]
         + sent * 2
         + [
             dma((4,)),

time: 42.4 us -> 41.4 us (0.976)
  Pallas kernels: 39.7 us -> 38.7 us
    pallas_call x1, Pallas kernels: 39.7 us -> 38.7 us  [per_device(): pl.pallas_call(kernel, out_shape=(jax.ShapeDtypeStruct((CHANNELS, beads),...]
where the time goes in v2:
time: 41.4 us; the launch traced here: 41.2 us
  Pallas kernels  38.7 us (93%)
  local copies, waits for them, and re-layouts  1.91 us (5%)
  between operations  0.65 us (2%)
    pallas_call x1, Pallas kernels, per_device(): pl.pallas_call(kernel, out_shape=(jax.ShapeDtypeStruct((CHANNELS, beads),...  38.7 us
    unnamed x4, local copies, waits for them, and re-layouts  1.91 us

profile of v2, /device:TPU:1, one launch (start us, length us, event | category | flops | bytes accessed | tf_op | source)
XLA Modules:
  0.0 41.2 jit_solution(3882036389158044804)
XLA Ops:
  0.6 38.7 %shard_map.59 = (f32[32,128]{1,0:T(8,128)}, f32[3,128]{1,0:T(4,128)}) custom-call(s32[3,1024]{1,0:T(4,128)} %mil.1, s32[3,128]{1,0:T(4,128)} %pos.1, f32[32,128]{1,0:T(8,128)} %wts.1, f32[32,1024]{1,0:T(8,128)} %obs.1), custom_call_target="tpu_custom_call" | custom-call | tf_op jit(solution)/shard_map/pallas_call | solution.py:373
  39.3 0.0 copy-start
  39.3 1.3 %copy.8 = f32[32,128]{1,0:T(8,128)} copy(f32[32,128]{1,0:T(8,128)} %get-tuple-element.4) | data formatting | bytes 32768
  40.7 0.0 copy-done
  40.7 0.6 %copy.9 = f32[3,128]{1,0:T(4,128)} copy(f32[3,128]{1,0:T(4,128)S(1)} %copy-done) | data formatting | bytes 3072
Async XLA Ops:
  39.3 1.3 %copy-start = (f32[3,128]{1,0:T(4,128)S(1)}, f32[3,128]{1,0:T(4,128)}, u32[]{:S(2)}) copy-start(f32[3,128]{1,0:T(4,128)} %get-tuple-element.5) | copy-start | bytes 4612

commit v3 on v2

--- a/solution.py
+++ b/solution.py
@@ -18,7 +18,6 @@
 F32 = jnp.float32
 
 SIN_POLY = (4.442883014678955, -7.308241367340088, 3.6062889099121094, -0.8457635641098022, 0.10920574516057968)
-COS_POLY = (1.4142135381698608, -6.978850841522217, 5.7394609451293945, -1.8835629224777222, 0.31069815158843994)
 
 SHARERS = 8
 REDUCERS = 32
@@ -30,6 +29,12 @@
 NN = (((1,), (0,)), ((), ()))
 
 
+FAR_FIRST = sorted(
+    ((dy, dz) for dy in range(4) for dz in range(8) if dy or dz),
+    key=lambda step: -min(step[0], 4 - step[0]) - min(step[1], 8 - step[1]),
+)
+
+
 def poly(u, coefs):
     total = u * coefs[-1] + coefs[-2]
     for c in coefs[-3::-1]:
@@ -41,8 +46,9 @@
     f = turns - jnp.round(turns)
     u = f * f
     s = poly(u, SIN_POLY) * f
-    c = poly(u, COS_POLY)
-    return 1.0 - s * s, s * c
+    square = s * s
+    rest = jnp.maximum(2.0 - square, 1e-30)
+    return 1.0 - square, s * (rest * lax.rsqrt(rest))
 
 
 def split(x):
@@ -55,10 +61,10 @@
 
 
 def kernel(
-    mil, pos, wts, obs, gw_out, gp_out,
+    mil, pos, wts, obs, gw_recv, gp_recv,
     mil_own, mil_use, pos_own, obs_own, obs_row, obs_send, posbuf, wbuf, mil_rows, pos_t, wsplit,
     hi_a, lo_a, hi_b, lo_b, phase,
-    amps, shares, coefs, left, grads, gw_send, gp_send, gw_recv, gp_recv,
+    amps, shares, coefs, left, grads, gw_send, gp_send,
     in_sem, a_send, a_recv, m_send, m_recv, r_send, r_recv, c_send, c_recv, d_send, d_recv,
     ready, met,
 ):
@@ -78,6 +84,10 @@
         y, z = r // 8, lax.rem(r, 8)
         return (lax.rem(z, 2) * 4 + x, (y * 4 + z // 2) * 2 + to_core)
 
+    def others():
+        for dy, dz in FAR_FIRST:
+            yield lax.rem(channel // 8 + dy, 4) * 8 + lax.rem(channel + dz, 8)
+
     def remote(src, dst, send, recv, device):
         return pltpu.make_async_remote_copy(
             src_ref=src, dst_ref=dst, send_sem=send, recv_sem=recv, device_id=device, device_id_type=MESH
@@ -106,6 +116,8 @@
     ]
     for copy in inputs:
         copy.start()
+    for s in range(1, REDUCERS):
+        greet(reducer(lax.rem(channel + s, REDUCERS), 1))
     for copy in inputs:
         copy.wait()
 
@@ -162,8 +174,6 @@
 
     for s in range(1, SHARERS):
         wts_copy(s).start()
-    for s in range(1, REDUCERS):
-        greet(reducer(lax.rem(channel + s, REDUCERS), 1))
 
     @pl.when(core != z_low)
     def _():
@@ -171,10 +181,6 @@
 
     index = mil_use[...].astype(F32)
     mil_rows[...] = jnp.concatenate([index, index, jnp.zeros((2, waves), F32)], 0).astype(BF16)
-
-    for s in range(1, SHARERS):
-        pos_copy(s).wait_recv()
-    pos_t[...] = posbuf[...].T.astype(BF16)
 
     sets = ((hi_a, lo_a), (hi_b, lo_b))
     rows = 32
@@ -194,61 +200,66 @@
 
     def add(q, turn, base):
         hi, lo = sets[turn]
-        at = pl.ds(base, 2 * CHUNK)
+        at = slice(base, base + 2 * CHUNK)
         both = dot(wsplit[...], hi[:, at], NN)
         amp = both[:CHANNELS] + both[CHANNELS:] + dot(wsplit[:CHANNELS, :], lo[:, at], NN)
         for t in range(PIECE):
             amps[q, pl.ds(t, REDUCERS, stride=PIECE), :] = amp[:, t * 128 : (t + 1) * 128]
 
-    def make(q, turn, base):
+    def make(q, turn, base, first=0, count=SHARERS * beads):
         hi, lo = sets[turn]
-        phase[...] = dot(pos_t[...], mil_rows[:, pl.ds(pl.multiple_of(q * CHUNK, CHUNK), CHUNK)], NN)
-        for r in range(0, phase.shape[0], rows):
+        phase[0:count, :] = dot(pos_t[pl.ds(first, count), :], mil_rows[:, q * CHUNK : (q + 1) * CHUNK], NN)
+        for r in range(0, count, rows):
+            to = pl.ds(first + r, rows) if isinstance(first, int) else pl.ds(pl.multiple_of(first + r, rows), rows)
             for part, value in enumerate(cos_sin(phase[r : r + rows, :])):
-                at = pl.ds(pl.multiple_of(base + part * CHUNK, CHUNK), CHUNK)
-                hi[r : r + rows, at], lo[r : r + rows, at] = split(value)
+                at = slice(base + part * CHUNK, base + (part + 1) * CHUNK)
+                hi[to, at], lo[to, at] = split(value)
 
     def send_shares(q):
-        for s in range(1, REDUCERS):
-            share_copy(q, channel, lax.rem(channel + s, REDUCERS)).start()
+        for r in others():
+            share_copy(q, channel, r).start()
         own_rows = pl.ds(pl.multiple_of(channel * PIECE, PIECE), PIECE)
         shares[q, own_rows, :] = amps[q, own_rows, :]
 
-    def forward(h, carry):
-        base = pl.multiple_of(h * 2 * CHUNK, 2 * CHUNK)
-        before = pl.multiple_of(jnp.maximum(h - 1, 0) * 2 * CHUNK, 2 * CHUNK)
-        add(lax.rem(2 * h + chunks - 1, chunks), 1, before)
-        make(2 * h, 0, base)
-
-        @pl.when(h > 0)
-        def _():
-            send_shares(2 * h - 1)
-
-        @pl.when(h == 0)
-        def _():
-            for s in range(1, SHARERS):
-                wts_copy(s).wait_recv()
-            high, low = split(wbuf[...])
-            wsplit[...] = jnp.concatenate([high, low], 0)
-
-        add(2 * h, 0, base)
-        make(2 * h + 1, 1, base)
-
-        @pl.when(jnp.logical_and(h == 0, core == 1))
-        def _():
-            pl.semaphore_wait(barrier, 2 * (REDUCERS - 1))
-            pl.semaphore_signal(met, inc=1, device_id=(kv, bead - 1), device_id_type=MESH)
-
-        @pl.when(jnp.logical_and(h == 0, core == 0))
-        def _():
-            pl.semaphore_wait(met, 1)
-
-        send_shares(2 * h)
-        return carry
-
-    lax.fori_loop(0, chunks // 2, forward, 0)
-    add(chunks - 1, 1, (chunks // 2 - 1) * 2 * CHUNK)
-    send_shares(chunks - 1)
+    for step in (0, 1, 3, 2):
+        chip = lax.rem(x + step, chips)
+        for c in range(2):
+            g = chip * 2 + c
+            shift = lax.rem(own - g + SHARERS, SHARERS)
+            if step:
+                pos_copy(shift).wait_recv()
+            else:
+
+                @pl.when(g != own)
+                def _():
+                    pos_copy(shift).wait_recv()
+
+        here = pl.multiple_of(chip * SLICE, SLICE)
+        pos_t[pl.ds(here, SLICE), :] = posbuf[:, pl.ds(here, SLICE)].T.astype(BF16)
+        make(0, 0, 0, here, SLICE)
+
+    for s in range(1, SHARERS):
+        wts_copy(s).wait_recv()
+    high, low = split(wbuf[...])
+    wsplit[...] = jnp.concatenate([high, low], 0)
+
+    for q in range(chunks):
+        base = (q // 2) * 2 * CHUNK
+        add(q, q % 2, base)
+        if q + 1 < chunks:
+            make(q + 1, (q + 1) % 2, ((q + 1) // 2) * 2 * CHUNK)
+        if q == 0:
+
+            @pl.when(core == 1)
+            def _():
+                pl.semaphore_wait(barrier, 2 * (REDUCERS - 1))
+                pl.semaphore_signal(met, inc=1, device_id=(kv, bead - 1), device_id_type=MESH)
+
+            @pl.when(core == 0)
+            def _():
+                pl.semaphore_wait(met, 1)
+
+        send_shares(q)
 
     @pl.when(core != z_low)
     def _():
@@ -268,8 +279,8 @@
         scale = residual * (2.0 / bead_total)
         own_rows = pl.ds(pl.multiple_of(channel * PIECE, PIECE), PIECE)
         coefs[q, own_rows, :] = jnp.concatenate([scale * amp_cos, scale * amp_sin], 0)
-        for s in range(1, REDUCERS):
-            coef_copy(q, lax.rem(channel + s, REDUCERS)).start()
+        for r in others():
+            coef_copy(q, r).start()
         return carry
 
     lax.fori_loop(0, chunks, coefficients, 0)
@@ -335,16 +346,17 @@
     for h in range(chunks // 2):
         backward(h)
 
-    gw_recv[own] = gw_send[own]
-    gp_recv[own] = gp_send[own]
+    kept = [
+        pltpu.make_async_copy(gw_send.at[own], gw_recv.at[own], in_sem.at[0]),
+        pltpu.make_async_copy(gp_send.at[own], gp_recv.at[own], in_sem.at[1]),
+    ]
+    for copy in kept:
+        copy.start()
     for s in range(1, SHARERS):
         for copy in sum_copies(lax.rem(own + s, SHARERS), s):
             copy.wait_recv()
-    gw, gp = gw_recv[0], gp_recv[0]
-    for g in range(1, SHARERS):
-        gw, gp = gw + gw_recv[g], gp + gp_recv[g]
-    gw_out[...] = gw
-    gp_out[...] = gp[:3]
+    for copy in kept:
+        copy.wait()
 
     for s in range(1, SHARERS):
         pos_copy(s).wait_send()
@@ -359,6 +371,14 @@
     def _():
         mil_copy.wait_send()
         obs_copy.wait_send()
+
+
+def total_kernel(gw_parts, gp_parts, gw_out, gp_out):
+    gw, gp = gw_parts[0], gp_parts[0]
+    for g in range(1, SHARERS):
+        gw, gp = gw + gw_parts[g], gp + gp_parts[g]
+    gw_out[...] = gw
+    gp_out[...] = gp[:3]
 
 
 def per_device(miller, lattice_pos, weights, observed):
@@ -370,14 +390,14 @@
     dma = pltpu.SemaphoreType.DMA
     pieces = pltpu.VMEM((chunks, REDUCERS * PIECE, 128), F32)
     sent = [pltpu.VMEM((SHARERS, CHANNELS, beads), F32), pltpu.VMEM((SHARERS, 4, beads), F32)]
-    return pl.pallas_call(
+    parts = pl.pallas_call(
         kernel,
         out_shape=(
-            jax.ShapeDtypeStruct((CHANNELS, beads), F32),
-            jax.ShapeDtypeStruct((3, beads), F32),
+            jax.ShapeDtypeStruct((SHARERS, CHANNELS, beads), F32),
+            jax.ShapeDtypeStruct((SHARERS, 4, beads), F32),
         ),
         in_specs=[hbm] * 4,
-        out_specs=[vmem] * 2,
+        out_specs=[hbm] * 2,
         scratch_shapes=[
             pltpu.VMEM(miller.shape, jnp.int32),
             pltpu.VMEM(miller.shape, jnp.int32),
@@ -395,7 +415,7 @@
         + [pltpu.VMEM((many, CHUNK), F32)]
         + [pieces] * 3
         + [pltpu.VMEM((8 * CHANNELS, 4 * CHUNK), BF16), pltpu.VMEM((4 * CHANNELS, many), F32)]
-        + sent * 2
+        + sent
         + [
             dma((4,)),
             dma((2, SHARERS)),
@@ -415,6 +435,15 @@
             collective_id=0, has_side_effects=True, vmem_limit_bytes=56 * 1024 * 1024
         ),
     )(miller, lattice_pos, weights, observed)
+    return pl.pallas_call(
+        total_kernel,
+        out_shape=(
+            jax.ShapeDtypeStruct((CHANNELS, beads), F32),
+            jax.ShapeDtypeStruct((3, beads), F32),
+        ),
+        in_specs=[vmem] * 2,
+        out_specs=[vmem] * 2,
+    )(*parts)
 
 
 def solution(mesh):

time: 41.4 us -> 39.7 us (0.959)
  local copies, waits for them, and re-layouts: 1.91 us -> 0 us
    unnamed x4 -> x0, local copies, waits for them, and re-layouts: 1.91 us -> none
    pallas_call x1 -> x2, Pallas kernels: 38.7 us -> 38.9 us  [the longest x1 37.4 us: per_device(): pl.pallas_call(kernel, out_shape=(jax.ShapeDtypeStruct((SHARERS, CHANNELS...]
where the time goes in v3:
time: 39.7 us; the launch traced here: 39.6 us
  Pallas kernels  38.9 us (98%)
  between operations  0.64 us (2%)
    pallas_call x1, Pallas kernels, per_device(): pl.pallas_call(kernel, out_shape=(jax.ShapeDtypeStruct((SHARERS, CHANNELS...  37.4 us
    pallas_call x1, Pallas kernels, per_device(): pl.pallas_call(total_kernel, out_shape=(jax.ShapeDtypeStruct((CHANNELS, b...  1.53 us

profile of v3, /device:TPU:1, one launch (start us, length us, event | category | flops | bytes accessed | tf_op | source)
XLA Modules:
  0.0 39.6 jit_solution(4096614602015963882)
XLA Ops:
  0.6 37.4 %shard_map.59 = (f32[8,32,128]{2,1,0:T(8,128)}, f32[8,4,128]{2,1,0:T(4,128)}) custom-call(s32[3,1024]{1,0:T(4,128)} %mil.1, s32[3,128]{1,0:T(4,128)} %pos.1, f32[32,128]{1,0:T(8,128)} %wts.1, f32[32,1024]{1,0:T(8,128)} %obs.1), custom_call_target="tpu_custom_call" | custom-call | tf_op jit(solution)/shard_map/pallas_call | solution.py:393
  38.0 1.5 %shard_map.60 = (f32[32,128]{1,0:T(8,128)}, f32[3,128]{1,0:T(4,128)}) custom-call(f32[8,32,128]{2,1,0:T(8,128)} %get-tuple-element.4.gw_parts, f32[8,4,128]{2,1,0:T(4,128)} %get-tuple-element.5.gp_parts), custom_call_target="tpu_custom_call" | custom-call | tf_op jit(solution)/shard_map/pallas_call | solution.py:438

commit v4 on v3

--- a/solution.py
+++ b/solution.py
@@ -17,14 +17,17 @@
 BF16 = jnp.bfloat16
 F32 = jnp.float32
 
-SIN_POLY = (4.442883014678955, -7.308241367340088, 3.6062889099121094, -0.8457635641098022, 0.10920574516057968)
+SIN_POLY = (4.442867755889893, -7.307443618774414, 3.594788074493408, -0.784373939037323)
+COS_POLY = (1.4142135381698608, -6.978850841522217, 5.7394609451293945, -1.8835629224777222, 0.31069815158843994)
 
 SHARERS = 8
 REDUCERS = 32
-CHUNK = 256
+CHUNKS = (256, 256, 256, 256)
+STARTS = tuple(sum(CHUNKS[:q]) for q in range(len(CHUNKS)))
+BASES = tuple(2 * sum(CHUNKS[q % 2 : q : 2]) for q in range(len(CHUNKS)))
+GROUPS = ((0, 1), (2, 3))
 SLICE = 256
-TILES = CHUNK // 128
-PIECE = 2 * TILES
+PIECES = tuple(2 * size // 128 for size in CHUNKS)
 NT = (((1,), (1,)), ((), ()))
 NN = (((1,), (0,)), ((), ()))
 
@@ -46,9 +49,8 @@
     f = turns - jnp.round(turns)
     u = f * f
     s = poly(u, SIN_POLY) * f
-    square = s * s
-    rest = jnp.maximum(2.0 - square, 1e-30)
-    return 1.0 - square, s * (rest * lax.rsqrt(rest))
+    c = poly(u, COS_POLY)
+    return 1.0 - s * s, s * c
 
 
 def split(x):
@@ -74,7 +76,7 @@
     own = x * 2 + core
     channel = (bead // 8) * 8 + lax.rem(bead // 2, 4) * 2 + z_low
     waves, beads = mil_use.shape[1], pos.shape[1]
-    chunks = waves // CHUNK
+    chunks = len(CHUNKS)
     chips = SHARERS // 2
 
     def sharer(g):
@@ -185,41 +187,44 @@
     sets = ((hi_a, lo_a), (hi_b, lo_b))
     rows = 32
 
-    def share_copy(q, r, to):
-        src = amps.at[q, pl.ds(pl.multiple_of(to * PIECE, PIECE), PIECE), :]
-        dst = shares.at[q, pl.ds(pl.multiple_of(r * PIECE, PIECE), PIECE), :]
+    def piece_rows(q, r):
+        return pl.ds(pl.multiple_of(r * PIECES[q], PIECES[q]), PIECES[q])
+
+    def share_copy(q, to):
+        src, dst = amps.at[q, piece_rows(q, to), :], shares.at[q, piece_rows(q, channel), :]
         return remote(src, dst, r_send.at[q], r_recv.at[q], reducer(to, core))
 
     def coef_copy(q, to):
-        at = coefs.at[q, pl.ds(pl.multiple_of(channel * PIECE, PIECE), PIECE), :]
+        at = coefs.at[q, piece_rows(q, channel), :]
         return remote(at, at, c_send.at[q], c_recv.at[q], reducer(to, core))
 
     def all_pieces(buf, q, send, recv):
-        at = buf.at[q, pl.ds(0, (REDUCERS - 1) * PIECE), :]
+        at = buf.at[q, pl.ds(0, (REDUCERS - 1) * PIECES[q]), :]
         return remote(at, at, send.at[q], recv.at[q], reducer(lax.rem(channel + 1, REDUCERS), core))
 
-    def add(q, turn, base):
-        hi, lo = sets[turn]
-        at = slice(base, base + 2 * CHUNK)
+    def add(q):
+        hi, lo = sets[q % 2]
+        at = slice(BASES[q], BASES[q] + 2 * CHUNKS[q])
         both = dot(wsplit[...], hi[:, at], NN)
         amp = both[:CHANNELS] + both[CHANNELS:] + dot(wsplit[:CHANNELS, :], lo[:, at], NN)
-        for t in range(PIECE):
-            amps[q, pl.ds(t, REDUCERS, stride=PIECE), :] = amp[:, t * 128 : (t + 1) * 128]
-
-    def make(q, turn, base, first=0, count=SHARERS * beads):
-        hi, lo = sets[turn]
-        phase[0:count, :] = dot(pos_t[pl.ds(first, count), :], mil_rows[:, q * CHUNK : (q + 1) * CHUNK], NN)
+        for t in range(PIECES[q]):
+            amps[q, pl.ds(t, REDUCERS, stride=PIECES[q]), :] = amp[:, t * 128 : (t + 1) * 128]
+
+    def make(q, first=0, count=SHARERS * beads):
+        (hi, lo), size = sets[q % 2], CHUNKS[q]
+        phase[0:count, 0:size] = dot(
+            pos_t[pl.ds(first, count), :], mil_rows[:, STARTS[q] : STARTS[q] + size], NN
+        )
         for r in range(0, count, rows):
             to = pl.ds(first + r, rows) if isinstance(first, int) else pl.ds(pl.multiple_of(first + r, rows), rows)
-            for part, value in enumerate(cos_sin(phase[r : r + rows, :])):
-                at = slice(base + part * CHUNK, base + (part + 1) * CHUNK)
+            for part, value in enumerate(cos_sin(phase[r : r + rows, 0:size])):
+                at = slice(BASES[q] + part * size, BASES[q] + (part + 1) * size)
                 hi[to, at], lo[to, at] = split(value)
 
     def send_shares(q):
         for r in others():
-            share_copy(q, channel, r).start()
-        own_rows = pl.ds(pl.multiple_of(channel * PIECE, PIECE), PIECE)
-        shares[q, own_rows, :] = amps[q, own_rows, :]
+            share_copy(q, r).start()
+        shares[q, piece_rows(q, channel), :] = amps[q, piece_rows(q, channel), :]
 
     for step in (0, 1, 3, 2):
         chip = lax.rem(x + step, chips)
@@ -236,7 +241,8 @@
 
         here = pl.multiple_of(chip * SLICE, SLICE)
         pos_t[pl.ds(here, SLICE), :] = posbuf[:, pl.ds(here, SLICE)].T.astype(BF16)
-        make(0, 0, 0, here, SLICE)
+        for q in range(1 if step else chunks):
+            make(q, here, SLICE)
 
     for s in range(1, SHARERS):
         wts_copy(s).wait_recv()
@@ -244,10 +250,10 @@
     wsplit[...] = jnp.concatenate([high, low], 0)
 
     for q in range(chunks):
-        base = (q // 2) * 2 * CHUNK
-        add(q, q % 2, base)
+        add(q)
         if q + 1 < chunks:
-            make(q + 1, (q + 1) % 2, ((q + 1) // 2) * 2 * CHUNK)
+            for step in (1, 3, 2):
+                make(q + 1, pl.multiple_of(lax.rem(x + step, chips) * SLICE, SLICE), SLICE)
         if q == 0:
 
             @pl.when(core == 1)
@@ -267,23 +273,20 @@
 
     bead_total = float(BEADS)
 
-    def coefficients(q, carry):
+    for q in range(chunks):
         all_pieces(shares, q, r_send, r_recv).wait_recv()
+        rows_in, tiles = PIECES[q], CHUNKS[q] // 128
         total = shares[q, 0:8, :]
-        for r in range(8, REDUCERS * PIECE, 8):
+        for r in range(8, REDUCERS * rows_in, 8):
             total = total + shares[q, r : r + 8, :]
-        total = total[:PIECE] + total[PIECE:]
-        amp_cos, amp_sin = total[:TILES], total[TILES:]
-        measured = obs_row[pl.ds(q * TILES, TILES), :]
+        total = sum(total[r : r + rows_in] for r in range(0, 8, rows_in))
+        amp_cos, amp_sin = total[:tiles], total[tiles:]
+        measured = obs_row[STARTS[q] // 128 : STARTS[q] // 128 + tiles, :]
         residual = (amp_cos * amp_cos + amp_sin * amp_sin) * (1.0 / bead_total) - measured
         scale = residual * (2.0 / bead_total)
-        own_rows = pl.ds(pl.multiple_of(channel * PIECE, PIECE), PIECE)
-        coefs[q, own_rows, :] = jnp.concatenate([scale * amp_cos, scale * amp_sin], 0)
+        coefs[q, piece_rows(q, channel), :] = jnp.concatenate([scale * amp_cos, scale * amp_sin], 0)
         for r in others():
             coef_copy(q, r).start()
-        return carry
-
-    lax.fori_loop(0, chunks, coefficients, 0)
 
     wide = 4 * CHANNELS
 
@@ -294,34 +297,40 @@
             remote(gp_send.at[g], gp_recv.at[own], d_send.at[1, s], d_recv.at[1, s], device),
         )
 
-    def backward(h):
-        for q in (2 * h, 2 * h + 1):
+    def backward(group):
+        filled = 0
+        for q in group:
             all_pieces(coefs, q, c_send, c_recv).wait_recv()
-            for t in range(TILES):
-                at = slice(q * CHUNK + t * 128, q * CHUNK + (t + 1) * 128)
-                co = coefs[q, pl.ds(t, CHANNELS, stride=PIECE), :]
-                si = coefs[q, pl.ds(TILES + t, CHANNELS, stride=PIECE), :]
+            tiles = CHUNKS[q] // 128
+            for t in range(tiles):
+                at = slice(STARTS[q] + t * 128, STARTS[q] + (t + 1) * 128)
+                co = coefs[q, pl.ds(t, CHANNELS, stride=PIECES[q]), :]
+                si = coefs[q, pl.ds(tiles + t, CHANNELS, stride=PIECES[q]), :]
                 vec = mil_use[:, at].astype(F32) * (TWO_PI / BOX_LEN)
                 for d in range(4):
                     lc, ls = (co, si) if d == 0 else (vec[d - 1 : d] * si, -vec[d - 1 : d] * co)
                     for part, value in ((0, lc), (1, ls)):
                         hi, lo = split(value)
-                        first = (2 * (q - 2 * h) + part) * CHUNK + t * 128
+                        first = filled + part * CHUNKS[q] + t * 128
                         to = slice(first, first + 128)
                         left[d * CHANNELS : (d + 1) * CHANNELS, to] = hi
                         left[(4 + d) * CHANNELS : (5 + d) * CHANNELS, to] = lo
-
-        span = slice(h * 2 * CHUNK, (h + 1) * 2 * CHUNK)
+            filled += 2 * CHUNKS[q]
+
+        def held(part, at):
+            return jnp.concatenate(
+                [sets[q % 2][part][at, BASES[q] : BASES[q] + 2 * CHUNKS[q]] for q in group], 1
+            )
 
         def one_chip(i, carry):
             chip = lax.rem(x + 1 + i, chips)
             at = pl.ds(pl.multiple_of(chip * SLICE, SLICE), SLICE)
-            both = dot(left[...], jnp.concatenate([hi_a[at, span], hi_b[at, span]], 1), NT)
-            rest = dot(left[:wide, :], jnp.concatenate([lo_a[at, span], lo_b[at, span]], 1), NT)
+            both = dot(left[:, :filled], held(0, at), NT)
+            rest = dot(left[:wide, :filled], held(1, at), NT)
             total = both[:wide] + both[wide:] + rest
-            if h > 0:
+            if group[0] > 0:
                 total = total + grads[:, at]
-            if h < chunks // 2 - 1:
+            if group[-1] < chunks - 1:
                 grads[:, at] = total
                 return carry
             weight = wbuf[:, at]
@@ -343,8 +352,8 @@
 
         lax.fori_loop(0, chips, one_chip, 0)
 
-    for h in range(chunks // 2):
-        backward(h)
+    for group in GROUPS:
+        backward(group)
 
     kept = [
         pltpu.make_async_copy(gw_send.at[own], gw_recv.at[own], in_sem.at[0]),
@@ -384,11 +393,12 @@
 def per_device(miller, lattice_pos, weights, observed):
     waves, beads = miller.shape[1], lattice_pos.shape[1]
     many = SHARERS * beads
-    chunks = waves // CHUNK
+    chunks = len(CHUNKS)
+    assert sum(CHUNKS) == waves
     hbm = pl.BlockSpec(memory_space=pltpu.HBM)
     vmem = pl.BlockSpec(memory_space=pltpu.VMEM)
     dma = pltpu.SemaphoreType.DMA
-    pieces = pltpu.VMEM((chunks, REDUCERS * PIECE, 128), F32)
+    pieces = pltpu.VMEM((chunks, REDUCERS * max(PIECES), 128), F32)
     sent = [pltpu.VMEM((SHARERS, CHANNELS, beads), F32), pltpu.VMEM((SHARERS, 4, beads), F32)]
     parts = pl.pallas_call(
         kernel,
@@ -411,10 +421,10 @@
             pltpu.VMEM((many, 8), BF16),
             pltpu.VMEM((2 * CHANNELS, many), BF16),
         ]
-        + [pltpu.VMEM((many, waves), BF16)] * 4
-        + [pltpu.VMEM((many, CHUNK), F32)]
+        + [pltpu.VMEM((many, 2 * sum(CHUNKS[turn::2])), BF16) for turn in (0, 0, 1, 1)]
+        + [pltpu.VMEM((many, max(CHUNKS)), F32)]
         + [pieces] * 3
-        + [pltpu.VMEM((8 * CHANNELS, 4 * CHUNK), BF16), pltpu.VMEM((4 * CHANNELS, many), F32)]
+        + [pltpu.VMEM((8 * CHANNELS, max(2 * sum(CHUNKS[q] for q in group) for group in GROUPS)), BF16), pltpu.VMEM((4 * CHANNELS, many), F32)]
         + sent
         + [
             dma((4,)),

time: 39.7 us -> 39.9 us (level)
  no operation moved by 1% of the time
where the time goes in v4:
time: 39.9 us; the launch traced here: 39.7 us
  Pallas kernels  39.1 us (98%)
  between operations  0.64 us (2%)
    pallas_call x1, Pallas kernels, per_device(): pl.pallas_call(kernel, out_shape=(jax.ShapeDtypeStruct((SHARERS, CHANNELS...  37.6 us
    pallas_call x1, Pallas kernels, per_device(): pl.pallas_call(total_kernel, out_shape=(jax.ShapeDtypeStruct((CHANNELS, b...  1.53 us

profile of v4, /device:TPU:1, one launch (start us, length us, event | category | flops | bytes accessed | tf_op | source)
XLA Modules:
  0.0 39.7 jit_solution(17334727774027410732)
XLA Ops:
  0.6 37.6 %shard_map.59 = (f32[8,32,128]{2,1,0:T(8,128)}, f32[8,4,128]{2,1,0:T(4,128)}) custom-call(s32[3,1024]{1,0:T(4,128)} %mil.1, s32[3,128]{1,0:T(4,128)} %pos.1, f32[32,128]{1,0:T(8,128)} %wts.1, f32[32,1024]{1,0:T(8,128)} %obs.1), custom_call_target="tpu_custom_call" | custom-call | tf_op jit(solution)/shard_map/pallas_call | solution.py:403
  38.2 1.5 %shard_map.60 = (f32[32,128]{1,0:T(8,128)}, f32[3,128]{1,0:T(4,128)}) custom-call(f32[8,32,128]{2,1,0:T(8,128)} %get-tuple-element.4.gw_parts, f32[8,4,128]{2,1,0:T(4,128)} %get-tuple-element.5.gp_parts), custom_call_target="tpu_custom_call" | custom-call | tf_op jit(solution)/shard_map/pallas_call | solution.py:448

commit v5 on v4

--- a/solution.py
+++ b/solution.py
@@ -17,8 +17,7 @@
 BF16 = jnp.bfloat16
 F32 = jnp.float32
 
-SIN_POLY = (4.442867755889893, -7.307443618774414, 3.594788074493408, -0.784373939037323)
-COS_POLY = (1.4142135381698608, -6.978850841522217, 5.7394609451293945, -1.8835629224777222, 0.31069815158843994)
+SIN_POLY = (2.641753911972046, -1.0863758325576782, 0.13399836421012878, -0.0077232783660292625)
 
 SHARERS = 8
 REDUCERS = 32
@@ -47,10 +46,12 @@
 
 def cos_sin(turns):
     f = turns - jnp.round(turns)
-    u = f * f
-    s = poly(u, SIN_POLY) * f
-    c = poly(u, COS_POLY)
-    return 1.0 - s * s, s * c
+    quarter = poly(f * f, SIN_POLY) * f
+    square = quarter * quarter
+    rest = 2.0 * math.sqrt(2.0) - square
+    half_sin = quarter * (rest * lax.rsqrt(rest))
+    half_cos = math.sqrt(2.0) - square
+    return 1.0 - half_sin * half_sin, half_sin * half_cos
 
 
 def split(x):

time: 39.9 us -> 39.8 us (level)
  no operation moved by 1% of the time
where the time goes in v5:
time: 39.8 us; the launch traced here: 39.7 us
  Pallas kernels  39 us (98%)
  between operations  0.64 us (2%)
    pallas_call x1, Pallas kernels, per_device(): pl.pallas_call(kernel, out_shape=(jax.ShapeDtypeStruct((SHARERS, CHANNELS...  37.5 us
    pallas_call x1, Pallas kernels, per_device(): pl.pallas_call(total_kernel, out_shape=(jax.ShapeDtypeStruct((CHANNELS, b...  1.53 us

profile of v5, /device:TPU:1, one launch (start us, length us, event | category | flops | bytes accessed | tf_op | source)
XLA Modules:
  0.0 39.7 jit_solution(1968573591522452267)
XLA Ops:
  0.6 37.5 %shard_map.59 = (f32[8,32,128]{2,1,0:T(8,128)}, f32[8,4,128]{2,1,0:T(4,128)}) custom-call(s32[3,1024]{1,0:T(4,128)} %mil.1, s32[3,128]{1,0:T(4,128)} %pos.1, f32[32,128]{1,0:T(8,128)} %wts.1, f32[32,1024]{1,0:T(8,128)} %obs.1), custom_call_target="tpu_custom_call" | custom-call | tf_op jit(solution)/shard_map/pallas_call | solution.py:404
  38.1 1.5 %shard_map.60 = (f32[32,128]{1,0:T(8,128)}, f32[3,128]{1,0:T(4,128)}) custom-call(f32[8,32,128]{2,1,0:T(8,128)} %get-tuple-element.4.gw_parts, f32[8,4,128]{2,1,0:T(4,128)} %get-tuple-element.5.gp_parts), custom_call_target="tpu_custom_call" | custom-call | tf_op jit(solution)/shard_map/pallas_call | solution.py:449

commit v6 on v3

--- a/solution.py
+++ b/solution.py
@@ -17,7 +17,7 @@
 BF16 = jnp.bfloat16
 F32 = jnp.float32
 
-SIN_POLY = (4.442883014678955, -7.308241367340088, 3.6062889099121094, -0.8457635641098022, 0.10920574516057968)
+SIN_POLY = (2.641753911972046, -1.0863758325576782, 0.13399836421012878, -0.0077232783660292625)
 
 SHARERS = 8
 REDUCERS = 32
@@ -44,11 +44,12 @@
 
 def cos_sin(turns):
     f = turns - jnp.round(turns)
-    u = f * f
-    s = poly(u, SIN_POLY) * f
-    square = s * s
-    rest = jnp.maximum(2.0 - square, 1e-30)
-    return 1.0 - square, s * (rest * lax.rsqrt(rest))
+    quarter = poly(f * f, SIN_POLY) * f
+    square = quarter * quarter
+    rest = 2.0 * math.sqrt(2.0) - square
+    half_sin = quarter * (rest * lax.rsqrt(rest))
+    half_cos = math.sqrt(2.0) - square
+    return 1.0 - half_sin * half_sin, half_sin * half_cos
 
 
 def split(x):

time: 39.7 us -> 39.7 us (level)
  no operation moved by 1% of the time
where the time goes in v6:
time: 39.7 us; the launch traced here: 39.6 us
  Pallas kernels  39 us (98%)
  between operations  0.64 us (2%)
    pallas_call x1, Pallas kernels, per_device(): pl.pallas_call(kernel, out_shape=(jax.ShapeDtypeStruct((SHARERS, CHANNELS...  37.4 us
    pallas_call x1, Pallas kernels, per_device(): pl.pallas_call(total_kernel, out_shape=(jax.ShapeDtypeStruct((CHANNELS, b...  1.53 us

profile of v6, /device:TPU:1, one launch (start us, length us, event | category | flops | bytes accessed | tf_op | source)
XLA Modules:
  0.0 39.6 jit_solution(2060247762881773430)
XLA Ops:
  0.6 37.4 %shard_map.59 = (f32[8,32,128]{2,1,0:T(8,128)}, f32[8,4,128]{2,1,0:T(4,128)}) custom-call(s32[3,1024]{1,0:T(4,128)} %mil.1, s32[3,128]{1,0:T(4,128)} %pos.1, f32[32,128]{1,0:T(8,128)} %wts.1, f32[32,1024]{1,0:T(8,128)} %obs.1), custom_call_target="tpu_custom_call" | custom-call | tf_op jit(solution)/shard_map/pallas_call | solution.py:394
  38.1 1.5 %shard_map.60 = (f32[32,128]{1,0:T(8,128)}, f32[3,128]{1,0:T(4,128)}) custom-call(f32[8,32,128]{2,1,0:T(8,128)} %get-tuple-element.4.gw_parts, f32[8,4,128]{2,1,0:T(4,128)} %get-tuple-element.5.gp_parts), custom_call_target="tpu_custom_call" | custom-call | tf_op jit(solution)/shard_map/pallas_call | solution.py:439

commit v7 on v6

--- a/solution.py
+++ b/solution.py
@@ -165,13 +165,13 @@
     mil_copy = remote(mil_own, mil_use, m_send.at[0], m_recv.at[0], beyond)
     obs_copy = remote(obs_send, obs_row, m_send.at[1], m_recv.at[1], beyond)
 
+    @pl.when(core == 0)
+    def _():
+        mil_copy.start()
+        obs_copy.start()
+
     for s in range(1, SHARERS):
         pos_copy(s).start()
-
-    @pl.when(core == 0)
-    def _():
-        mil_copy.start()
-        obs_copy.start()
 
     for s in range(1, SHARERS):
         wts_copy(s).start()

time: 39.7 us -> 39.7 us (level)
  no operation moved by 1% of the time
where the time goes in v7:
time: 39.7 us; the launch traced here: 39.6 us
  Pallas kernels  39 us (98%)
  between operations  0.64 us (2%)
    pallas_call x1, Pallas kernels, per_device(): pl.pallas_call(kernel, out_shape=(jax.ShapeDtypeStruct((SHARERS, CHANNELS...  37.4 us
    pallas_call x1, Pallas kernels, per_device(): pl.pallas_call(total_kernel, out_shape=(jax.ShapeDtypeStruct((CHANNELS, b...  1.53 us

profile of v7, /device:TPU:1, one launch (start us, length us, event | category | flops | bytes accessed | tf_op | source)
XLA Modules:
  0.0 39.6 jit_solution(5785681002156015089)
XLA Ops:
  0.6 37.4 %shard_map.59 = (f32[8,32,128]{2,1,0:T(8,128)}, f32[8,4,128]{2,1,0:T(4,128)}) custom-call(s32[3,1024]{1,0:T(4,128)} %mil.1, s32[3,128]{1,0:T(4,128)} %pos.1, f32[32,128]{1,0:T(8,128)} %wts.1, f32[32,1024]{1,0:T(8,128)} %obs.1), custom_call_target="tpu_custom_call" | custom-call | tf_op jit(solution)/shard_map/pallas_call | solution.py:394
  38.1 1.5 %shard_map.60 = (f32[32,128]{1,0:T(8,128)}, f32[3,128]{1,0:T(4,128)}) custom-call(f32[8,32,128]{2,1,0:T(8,128)} %get-tuple-element.4.gw_parts, f32[8,4,128]{2,1,0:T(4,128)} %get-tuple-element.5.gp_parts), custom_call_target="tpu_custom_call" | custom-call | tf_op jit(solution)/shard_map/pallas_call | solution.py:439
